TPU v7x, 32 devices: a whole 2x2x4 slice. The times are simulated.
32 devices in a mesh: group: 2 (over x), shard: 16 (over z, y, core).
Axes of the slice: x: 2, y: 2, z: 4, core: 2. Of those that a mesh axis runs over, the one named last changes fastest.
Arguments:
- offer_attribute_matrix: bfloat16 [128, 128, 1024], P(('group', 'shard')), may hold values from -6 to 6
- kept_offers: int32 [128, 32], P(('group', 'shard')), may hold values from 0 to 127, as said below
- expert_target: int32 [128, 6], P(('group', 'shard')), may hold values from 0 to 15, all different within a row; in each aligned block of 4 rows (0 to 3, 4 to 7, ...) at most 3 rows name the same one
- sequence_extent: int32 [128], P(('group', 'shard')), may hold values from 1 to 128
- behaviour_sequence: bfloat16 [128, 128, 512], P(('group', 'shard')), may hold values from -6 to 6
- inner_projection_matrix: bfloat16 [1024, 1024], replicated, may hold values from -0.1875 to 0.1875
- student_rating_vector: bfloat16 [1024], replicated, may hold values from -0.1875 to 0.1875
- asking_matrix: bfloat16 [16, 1024, 512], P('shard'), may hold values from -0.1875 to 0.1875
- lookup_matrix: bfloat16 [16, 512, 512], P('shard'), may hold values from -0.25 to 0.25
- content_matrix: bfloat16 [16, 512, 512], P('shard'), may hold values from -0.25 to 0.25
- expert_rating_vector: bfloat16 [16, 512], P('shard'), may hold values from -1.1953125 to 1.1953125
Outputs:
- grad_hidden: float32 [1024, 1024], P('shard')
- grad_score: float32 [1024], replicated
Inputs may be any that keep to these rules, and one draw needn't show every extreme that they name: `kept_offers`: the 32 survivors of a request are distinct candidates. `expert_target`: each request names 6 distinct experts; the requests of one device name any expert at most 3 times, a bound that some block reaches.
All inputs are finite; a program needn't handle non-finite values.
Results may differ from a plain program's by a relative error of at most 0.005.
Values may be sent and summed in bfloat16 or wider, within the bound.
No kernel may reach another device: no remote copies, remote signals or barrier semaphores. Data moves between devices by JAX's collectives and lax.ppermute only.
A program may use at most 128 MiB of HBM per device.

v0:
```python
import jax
import jax.numpy as jnp
from jax import lax
from jax.sharding import PartitionSpec as P

ATTENDER_GANGS = 8


def body(
    offer_attribute_matrix,
    kept_offers,
    expert_target,
    sequence_extent,
    behaviour_sequence,
    inner_projection_matrix,
    student_rating_vector,
    asking_matrix,
    lookup_matrix,
    content_matrix,
    expert_rating_vector,
):
    requests_here, offer_number, attribute_span = offer_attribute_matrix.shape
    kept_number = kept_offers.shape[1]
    hist_slots, focus_span = (behaviour_sequence.shape[1], behaviour_sequence.shape[2])
    rankers_each = expert_target.shape[1]
    ranker_count = lax.axis_size("shard")
    routed_rows = requests_here * rankers_each
    capacity = max(2, (routed_rows + ranker_count - 1) // ranker_count + 1)
    place_number = ranker_count * capacity
    row_dest = expert_target.reshape(routed_rows)
    by_expert = (row_dest[:, None] == jnp.arange(ranker_count, dtype=jnp.int32)[None, :]).astype(
        jnp.int32
    )
    earlier = jnp.cumsum(by_expert, axis=0) - by_expert
    rank_in = jnp.sum(earlier * by_expert, axis=1)
    slot_of = row_dest * capacity + rank_in
    placing = slot_of[:, None] == jnp.arange(place_number, dtype=jnp.int32)[None, :]
    placing = placing.reshape(requests_here, rankers_each, place_number)
    placing_b = placing.astype(jnp.bfloat16)
    placing_f = placing.astype(jnp.float32)
    chosen_lines = (
        kept_offers[:, :, None] == jnp.arange(offer_number, dtype=jnp.int32)[None, None, :]
    ).astype(jnp.bfloat16)
    chosen = jnp.einsum(
        "rkc,rcf->rkf", chosen_lines, offer_attribute_matrix, preferred_element_type=jnp.float32
    ).astype(jnp.bfloat16)
    send_rows = jnp.einsum(
        "rts,rkf->skf", placing_b, chosen, preferred_element_type=jnp.float32
    ).astype(jnp.bfloat16)
    send_hist = jnp.einsum(
        "rts,rjf->sjf", placing_b, behaviour_sequence, preferred_element_type=jnp.float32
    ).astype(jnp.bfloat16)
    send_len = jnp.einsum("rts,r->s", placing_f, sequence_extent.astype(jnp.float32)).astype(
        jnp.bfloat16
    )
    arriving_lines, recv_hist, recv_len = (
        lax.all_to_all(send_rows, "shard", split_axis=0, concat_axis=0, tiled=True),
        lax.all_to_all(send_hist, "shard", split_axis=0, concat_axis=0, tiled=True),
        lax.all_to_all(send_len, "shard", split_axis=0, concat_axis=0, tiled=True),
    )
    single_attender_span = focus_span // ATTENDER_GANGS
    segment_places = 16
    segment_number = place_number // segment_places

    def ranker_block(block):
        rows, hist_rows, lens = block
        queries = jnp.dot(
            rows.reshape(-1, attribute_span), asking_matrix[0], preferred_element_type=jnp.float32
        )
        queries = queries.astype(jnp.bfloat16).reshape(
            segment_places, kept_number, ATTENDER_GANGS, single_attender_span
        )
        flat_hist = hist_rows.reshape(-1, focus_span)
        key_rows = jnp.dot(flat_hist, lookup_matrix[0], preferred_element_type=jnp.float32)
        key_rows = key_rows.astype(jnp.bfloat16).reshape(
            segment_places, hist_slots, ATTENDER_GANGS, single_attender_span
        )
        value_rows = jnp.dot(flat_hist, content_matrix[0], preferred_element_type=jnp.float32)
        value_rows = value_rows.astype(jnp.bfloat16).reshape(
            segment_places, hist_slots, ATTENDER_GANGS, single_attender_span
        )
        logits = jnp.einsum(
            "skhd,sjhd->shkj", queries, key_rows, preferred_element_type=jnp.float32
        ) * single_attender_span ** (-0.5)
        lengths = jnp.maximum(lens.astype(jnp.float32), jnp.float32(1.0))
        visible = (
            jnp.arange(hist_slots, dtype=jnp.float32)[None, None, None, :]
            < lengths[:, None, None, None]
        )
        weights = jnp.where(visible, jnp.exp(logits), jnp.float32(0.0))
        attn_probs = (weights / jnp.sum(weights, axis=-1, keepdims=True)).astype(jnp.bfloat16)
        mixed_context = jnp.einsum(
            "shkj,sjhd->skhd", attn_probs, value_rows, preferred_element_type=jnp.float32
        )
        mixed_context = mixed_context.reshape(segment_places, kept_number, focus_span)
        return jnp.sum(mixed_context * expert_rating_vector[0].astype(jnp.float32), axis=-1)

    mentor_output = lax.map(
        ranker_block,
        (
            arriving_lines.reshape(segment_number, segment_places, kept_number, attribute_span),
            recv_hist.reshape(segment_number, segment_places, hist_slots, focus_span),
            recv_len.reshape(segment_number, segment_places),
        ),
    )
    mentor_output = mentor_output.reshape(place_number, kept_number)
    returned = lax.all_to_all(mentor_output, "shard", split_axis=0, concat_axis=0, tiled=True)
    own_teacher = (
        jnp.einsum("rts,sk->rk", placing_f, returned, precision=lax.Precision.HIGHEST)
        / rankers_each
    )
    score_vec = student_rating_vector.astype(jnp.float32)
    flat_feats = offer_attribute_matrix.reshape(requests_here * offer_number, attribute_span)
    preact = jnp.dot(flat_feats, inner_projection_matrix, preferred_element_type=jnp.float32)
    hidden = jnp.maximum(preact, jnp.float32(0.0))
    scores = jnp.sum(hidden * score_vec, axis=-1).reshape(requests_here, offer_number)
    exp_scores = jnp.exp(scores)
    student = exp_scores / jnp.sum(exp_scores, axis=-1, keepdims=True)
    exp_teacher = jnp.exp(own_teacher)
    target = exp_teacher / jnp.sum(exp_teacher, axis=-1, keepdims=True)
    target_cand = jnp.sum(target[:, :, None] * chosen_lines.astype(jnp.float32), axis=1)
    score_grad = (student - target_cand).reshape(requests_here * offer_number, 1)
    hidden_grad = (score_grad * score_vec * (preact > 0).astype(jnp.float32)).astype(jnp.bfloat16)
    local_score = jnp.sum(score_grad * hidden, axis=0)
    grad_rows = lax.psum_scatter(
        lax.dot_general(
            flat_feats, hidden_grad, (((0,), (0,)), ((), ())), preferred_element_type=jnp.float32
        ),
        "shard",
        scatter_dimension=0,
        tiled=True,
    )
    grad_hidden = lax.psum(grad_rows, "group")
    grad_score = lax.psum(local_score, ("group", "shard"))
    return (grad_hidden, grad_score)


def solution(mesh):
    placed = (
        P(("group", "shard"), None, None),
        P(("group", "shard"), None),
        P(("group", "shard"), None),
        P(("group", "shard")),
        P(("group", "shard"), None, None),
        P(),
        P(),
        P("shard", None, None),
        P("shard", None, None),
        P("shard", None, None),
        P("shard", None),
    )
    return jax.shard_map(
        body, mesh=mesh, in_specs=placed, out_specs=(P("shard", None), P()), check_vma=False
    )
```

profile of v0, /device:TPU:0, one launch (start us, length us, event | category | flops | bytes accessed | tf_op | source)
XLA Modules:
  0.0 495.7 jit_solution(17073846660387039856)
XLA Ops:
  10.8 7.4 %all-to-all-start.1 = ((bf16[16,3,1]{1,2,0:T(2,128)(2,1)}), bf16[16,3,1]{1,2,0:T(2,128)(2,1)S(1)}, u32[]{:S(2)}, u32[]{:S(2)}) async-start(bf16[16,3,1]{1,2,0:T(2,128)(2,1)} %all_to_all.27), calls=%async_computation.1 | async-start | bytes 16384 | tf_op jit(solution)/shard_map/all_to_all | solution.py:59
  24.6 5.8 %all-to-all-start.2 = ((bf16[48,32,1024]{2,1,0:T(8,128)(2,1)}), bf16[48,32,1024]{2,1,0:T(8,128)(2,1)}, u32[]{:S(2)}, u32[]{:S(2)}) async-start(bf16[48,32,1024]{2,1,0:T(8,128)(2,1)} %copy.50), calls=%async_computation.2 | async-start | bytes 6291456 | tf_op jit(solution)/shard_map/all_to_all | solution.py:57
  32.3 6.3 %copy.47 = bf16[48,128,512]{2,1,0:T(8,128)(2,1)} copy(bf16[48,128,512]{2,0,1:T(8,128)(2,1)S(1)} %convolution_convert_fusion.3) | data formatting | bytes 12582912 | tf_op jit(solution)/shard_map/convert_element_type | solution.py:52
  38.6 51.1 %all-to-all-done.2 = bf16[48,32,1024]{2,1,0:T(8,128)(2,1)} async-done(((bf16[48,32,1024]{2,1,0:T(8,128)(2,1)}), bf16[48,32,1024]{2,1,0:T(8,128)(2,1)}, u32[]{:S(2)}, u32[]{:S(2)}) %all-to-all-start.2) | async-done | bytes 3145760 | tf_op jit(solution)/shard_map/all_to_all | solution.py:57
  89.7 15.5 %all-to-all-start = ((bf16[48,128,512]{2,1,0:T(8,128)(2,1)}), bf16[48,128,512]{2,1,0:T(8,128)(2,1)}, u32[]{:S(2)}, u32[]{:S(2)}) async-start(bf16[48,128,512]{2,1,0:T(8,128)(2,1)} %copy.47), calls=%async_computation | async-start | bytes 12582912 | tf_op jit(solution)/shard_map/all_to_all | solution.py:58
  108.0 111.3 %all-to-all-done = bf16[48,128,512]{2,1,0:T(8,128)(2,1)} async-done(((bf16[48,128,512]{2,1,0:T(8,128)(2,1)}), bf16[48,128,512]{2,1,0:T(8,128)(2,1)}, u32[]{:S(2)}, u32[]{:S(2)}) %all-to-all-start) | async-done | bytes 6291488 | tf_op jit(solution)/shard_map/all_to_all | solution.py:58
  219.3 107.4 %while.10 = (s32[]{:T(128)}, f32[3,16,32]{2,1,0:T(8,128)S(1)}, bf16[3,16,128,512]{3,2,1,0:T(8,128)(2,1)}, bf16[1,512,512]{2,1,0:T(8,128)(2,1)}, bf16[3,16]{1,0:T...) while((s32[]{:T(128)}, f32[3,16,32]{2,1,0:T(8,128)S(1)}, ...), condition=%wide.region_9.10_spmd, body=%wide.region_6.9_spmd.sunk | while | flops 2825123840 | bytes 61932960 | solution.py:98
  225.1 6.2 %reshape.149 = bf16[16,128,8,64]{3,2,1,0:T(8,128)(2,1)} reshape(bf16[2048,512]{1,0:T(8,128)(2,1)} %convolution_convert_fusion.10) | data formatting | bytes 4194304 | tf_op jit(solution)/shard_map/while/body/eval_jaxpr/reshape | solution.py:75
  236.0 6.0 %fusion.64 = (f32[16,8,32]{2,1,0:T(8,128)S(1)}, f32[16,8,32,128]{3,2,1,0:T(8,128)}) fusion(pred[16,128]{1,0:T(8,128)(4,1)S(1)} %iota_compare_fusion.6, bf16[16,128,8,64]{3,2,1,0:T(8,128)(2,1)} %reshape.149, bf16[16,32,8,64]{3,2,1,0:T(8,128)(2,1)S(1)} %reshape.150), kind=kOutput, calls=%fused_computation.9.clone.1 | convolution fusion | flops 68677632 | bytes 4737024 | tf_op jit(solution)/shard_map/while/body/eval_jaxpr/skhd,sjhd->shkj/dot_general | solution.py:82
  244.6 6.2 %reshape.148 = bf16[16,128,8,64]{3,2,1,0:T(8,128)(2,1)} reshape(bf16[2048,512]{1,0:T(8,128)(2,1)} %convolution_convert_fusion.9) | data formatting | bytes 4194304 | tf_op jit(solution)/shard_map/while/body/eval_jaxpr/reshape | solution.py:79
  260.8 6.2 %reshape.149 = bf16[16,128,8,64]{3,2,1,0:T(8,128)(2,1)} reshape(bf16[2048,512]{1,0:T(8,128)(2,1)} %convolution_convert_fusion.10) | data formatting | bytes 4194304 | tf_op jit(solution)/shard_map/while/body/eval_jaxpr/reshape | solution.py:75
  271.8 6.0 %fusion.64 = (f32[16,8,32]{2,1,0:T(8,128)S(1)}, f32[16,8,32,128]{3,2,1,0:T(8,128)}) fusion(pred[16,128]{1,0:T(8,128)(4,1)S(1)} %iota_compare_fusion.6, bf16[16,128,8,64]{3,2,1,0:T(8,128)(2,1)} %reshape.149, bf16[16,32,8,64]{3,2,1,0:T(8,128)(2,1)S(1)} %reshape.150), kind=kOutput, calls=%fused_computation.9.clone.1 | convolution fusion | flops 68677632 | bytes 4737024 | tf_op jit(solution)/shard_map/while/body/eval_jaxpr/skhd,sjhd->shkj/dot_general | solution.py:82
  280.4 6.2 %reshape.148 = bf16[16,128,8,64]{3,2,1,0:T(8,128)(2,1)} reshape(bf16[2048,512]{1,0:T(8,128)(2,1)} %convolution_convert_fusion.9) | data formatting | bytes 4194304 | tf_op jit(solution)/shard_map/while/body/eval_jaxpr/reshape | solution.py:79
  286.6 4.2 multiply_reduce_fusion.5
  296.6 6.2 %reshape.149 = bf16[16,128,8,64]{3,2,1,0:T(8,128)(2,1)} reshape(bf16[2048,512]{1,0:T(8,128)(2,1)} %convolution_convert_fusion.10) | data formatting | bytes 4194304 | tf_op jit(solution)/shard_map/while/body/eval_jaxpr/reshape | solution.py:75
  307.6 6.0 %fusion.64 = (f32[16,8,32]{2,1,0:T(8,128)S(1)}, f32[16,8,32,128]{3,2,1,0:T(8,128)}) fusion(pred[16,128]{1,0:T(8,128)(4,1)S(1)} %iota_compare_fusion.6, bf16[16,128,8,64]{3,2,1,0:T(8,128)(2,1)} %reshape.149, bf16[16,32,8,64]{3,2,1,0:T(8,128)(2,1)S(1)} %reshape.150), kind=kOutput, calls=%fused_computation.9.clone.1 | convolution fusion | flops 68677632 | bytes 4737024 | tf_op jit(solution)/shard_map/while/body/eval_jaxpr/skhd,sjhd->shkj/dot_general | solution.py:82
  316.2 6.2 %reshape.148 = bf16[16,128,8,64]{3,2,1,0:T(8,128)(2,1)} reshape(bf16[2048,512]{1,0:T(8,128)(2,1)} %convolution_convert_fusion.9) | data formatting | bytes 4194304 | tf_op jit(solution)/shard_map/while/body/eval_jaxpr/reshape | solution.py:79
  322.4 4.2 multiply_reduce_fusion.5
  327.3 28.1 %all-to-all-start.3 = ((f32[16,3,32]{2,1,0:T(4,128)}), f32[16,3,32]{2,1,0:T(4,128)S(1)}, u32[]{:S(2)}, u32[]{:S(2)}) async-start(f32[16,3,32]{2,1,0:T(4,128)} %all_to_all.24), calls=%async_computation.3 | async-start | bytes 65536 | tf_op jit(solution)/shard_map/all_to_all | solution.py:107
  355.5 6.5 %all-to-all-done.3 = f32[16,3,32]{2,1,0:T(4,128)S(1)} async-done(((f32[16,3,32]{2,1,0:T(4,128)}), f32[16,3,32]{2,1,0:T(4,128)S(1)}, u32[]{:S(2)}, u32[]{:S(2)}) %all-to-all-start.3) | async-done | bytes 6176 | tf_op jit(solution)/shard_map/all_to_all | solution.py:107
  362.6 5.2 %convolution_bitcast_fusion = f32[1024,1024]{0,1:T(8,128)} fusion(bf16[512,1024]{1,0:T(8,128)(2,1)} %bitcast.74, f32[512,1024]{1,0:T(8,128)} %get-tuple-element.101, f32[512]{0:T(512)S(1)} %bitcast_subtract_fusion, f32[1024]{0:T(1024)S(1)} %convert_element_type.71), kind=kOutput, calls=%fused_computation.32 | convolution fusion | flops 1075838976 | bytes 7346176 | tf_op jit(solution)/shard_map/dot_general | solution.py:126
  367.8 5.3 %copy.56 = f32[1024,1024]{1,0:T(8,128)} copy(f32[1024,1024]{0,1:T(8,128)} %convolution_bitcast_fusion) | data formatting | bytes 8388608
  373.2 70.1 %reduce-scatter.4.cloned.1.call-done = f32[64,1024]{1,0:T(8,128)} async-done(((f32[1024,1024]{1,0:T(8,128)}), f32[64,1024]{1,0:T(8,128)}) %reduce-scatter.4.cloned.1.call-update) | async-done | bytes 262160
  447.2 39.8 %psum.15 = f32[1024]{0:T(1024)} all-reduce(f32[1024]{0:T(1024)S(1)} %multiply_reduce_fusion.1), channel_id=1, replica_groups=mesh['group'=2,'shard'=16] {'group','shard'}, use_global_device_ids=true, to_apply=%region_15.16 | all-reduce | flops 1024 | bytes 8192 | tf_op jit(solution)/shard_map/psum | solution.py:134
  (111 shorter events, 65.6 us)
Async XLA Ops:
  7.2 98.1 %copy-start = (bf16[1024,1024]{1,0:T(8,128)(2,1)S(1)}, bf16[1024,1024]{1,0:T(8,128)(2,1)}, u32[]{:S(2)}) copy-start(bf16[1024,1024]{1,0:T(8,128)(2,1)} %param.18) | copy-start | bytes 6291460
  10.8 13.8 %all-to-all-start.1 = ((bf16[16,3,1]{1,2,0:T(2,128)(2,1)}), bf16[16,3,1]{1,2,0:T(2,128)(2,1)S(1)}, u32[]{:S(2)}, u32[]{:S(2)}) async-start(bf16[16,3,1]{1,2,0:T(2,128)(2,1)} %all_to_all.27), calls=%async_computation.1 | async-start | bytes 16384 | tf_op jit(solution)/shard_map/all_to_all | solution.py:59
  24.2 6.2 %copy-start.4 = (bf16[4,128,512]{2,1,0:T(8,128)(2,1)S(1)}, bf16[4,128,512]{2,1,0:T(8,128)(2,1)}, u32[]{:S(2)}) copy-start(bf16[4,128,512]{2,1,0:T(8,128)(2,1)} %param.17) | copy-start | bytes 1572868
  24.6 65.1 %all-to-all-start.2 = ((bf16[48,32,1024]{2,1,0:T(8,128)(2,1)}), bf16[48,32,1024]{2,1,0:T(8,128)(2,1)}, u32[]{:S(2)}, u32[]{:S(2)}) async-start(bf16[48,32,1024]{2,1,0:T(8,128)(2,1)} %copy.50), calls=%async_computation.2 | async-start | bytes 6291456 | tf_op jit(solution)/shard_map/all_to_all | solution.py:57
  38.6 66.6 %copy-start.7 = (bf16[1024]{0:T(1024)(128)(2,1)S(1)}, bf16[1024]{0:T(1024)(128)(2,1)}, u32[]{:S(2)}) copy-start(bf16[1024]{0:T(1024)(128)(2,1)} %param.19) | copy-start | bytes 6148
  38.6 66.7 %copy-start.3 = (bf16[4,128,1024]{2,1,0:T(8,128)(2,1)S(1)}, bf16[4,128,1024]{2,1,0:T(8,128)(2,1)}, u32[]{:S(2)}) copy-start(bf16[4,128,1024]{2,1,0:T(8,128)(2,1)} %param.13) | copy-start | bytes 3145732
  89.7 129.5 %all-to-all-start = ((bf16[48,128,512]{2,1,0:T(8,128)(2,1)}), bf16[48,128,512]{2,1,0:T(8,128)(2,1)}, u32[]{:S(2)}, u32[]{:S(2)}) async-start(bf16[48,128,512]{2,1,0:T(8,128)(2,1)} %copy.47), calls=%async_computation | async-start | bytes 12582912 | tf_op jit(solution)/shard_map/all_to_all | solution.py:58
  105.3 114.0 %copy-start.5 = (bf16[1,512]{1,0:T(2,128)(2,1)S(1)}, bf16[1,512]{1,0:T(2,128)(2,1)}, u32[]{:S(2)}) copy-start(bf16[1,512]{1,0:T(2,128)(2,1)} %param.23) | copy-start | bytes 3076
  219.3 143.1 %copy-start.6 = (s32[4,32]{1,0:T(4,128)S(1)}, s32[4,32]{1,0:T(4,128)}, u32[]{:S(2)}) copy-start(s32[4,32]{1,0:T(4,128)} %param.14) | copy-start | bytes 1540
  219.3 3.2 copy-start.10
  231.2 1.5 copy-start.8
  236.0 6.0 %copy-start.2 = (bf16[1,16,128,512]{3,2,1,0:T(8,128)(2,1)S(1)}, bf16[1,16,128,512]{3,2,1,0:T(8,128)(2,1)}, u32[]{:S(2)}) copy-start(bf16[1,16,128,512]{3,2,1,0:T(8,128)(2,1)} %copy-done.1) | copy-start | bytes 6291460 | tf_op jit(solution)/shard_map/while
  236.0 6.0 %copy-start.9 = (bf16[1,512,512]{2,1,0:T(8,128)(2,1)S(1)}, bf16[1,512,512]{2,1,0:T(8,128)(2,1)}, u32[]{:S(2)}) copy-start(bf16[1,512,512]{2,1,0:T(8,128)(2,1)} %get-tuple-element.184) | copy-start | bytes 1572868 | tf_op jit(solution)/shard_map/while
  255.1 3.2 copy-start.10
  267.0 1.5 copy-start.8
  271.8 6.0 %copy-start.2 = (bf16[1,16,128,512]{3,2,1,0:T(8,128)(2,1)S(1)}, bf16[1,16,128,512]{3,2,1,0:T(8,128)(2,1)}, u32[]{:S(2)}) copy-start(bf16[1,16,128,512]{3,2,1,0:T(8,128)(2,1)} %copy-done.1) | copy-start | bytes 6291460 | tf_op jit(solution)/shard_map/while
  271.8 6.0 %copy-start.9 = (bf16[1,512,512]{2,1,0:T(8,128)(2,1)S(1)}, bf16[1,512,512]{2,1,0:T(8,128)(2,1)}, u32[]{:S(2)}) copy-start(bf16[1,512,512]{2,1,0:T(8,128)(2,1)} %get-tuple-element.184) | copy-start | bytes 1572868 | tf_op jit(solution)/shard_map/while
  290.9 3.2 copy-start.10
  302.8 1.5 copy-start.8
  307.6 6.0 %copy-start.2 = (bf16[1,16,128,512]{3,2,1,0:T(8,128)(2,1)S(1)}, bf16[1,16,128,512]{3,2,1,0:T(8,128)(2,1)}, u32[]{:S(2)}) copy-start(bf16[1,16,128,512]{3,2,1,0:T(8,128)(2,1)} %copy-done.1) | copy-start | bytes 6291460 | tf_op jit(solution)/shard_map/while
  307.6 6.0 %copy-start.9 = (bf16[1,512,512]{2,1,0:T(8,128)(2,1)S(1)}, bf16[1,512,512]{2,1,0:T(8,128)(2,1)}, u32[]{:S(2)}) copy-start(bf16[1,512,512]{2,1,0:T(8,128)(2,1)} %get-tuple-element.184) | copy-start | bytes 1572868 | tf_op jit(solution)/shard_map/while
  327.3 34.7 %all-to-all-start.3 = ((f32[16,3,32]{2,1,0:T(4,128)}), f32[16,3,32]{2,1,0:T(4,128)S(1)}, u32[]{:S(2)}, u32[]{:S(2)}) async-start(f32[16,3,32]{2,1,0:T(4,128)} %all_to_all.24), calls=%async_computation.3 | async-start | bytes 65536 | tf_op jit(solution)/shard_map/all_to_all | solution.py:107
  355.4 88.0 %reduce-scatter.4.cloned.1.call-start = ((), (), s32[]{:S(2)}) async-start(), calls=%async_computation.6 | async-start | bytes 4456448
  373.1 113.8 %all-reduce.2.cloned.1.call-start = ((), (), s32[]{:S(2)}) async-start(), calls=%async_computation.5 | async-start | bytes 1048576 | tf_op jit(solution)/shard_map/psum | solution.py:133
  (3 other events, 3.9 us)
Sparse Core Ops, SparseCore 0:
  373.3 70.0 reduce-scatter.3
  445.6 28.0 all-reduce.1
where the time goes:
time: 497 us; the launch traced here: 496 us
  waiting for transfers between devices  239 us (48%)
  local copies, waits for them, and re-layouts  77.7 us (16%)
  matrix products  63.9 us (13%)
  starting transfers between devices  56.9 us (11%)
  blocking collectives  39.8 us (8%)
  between operations  14.2 us (3%)
    all_to_all x1, waiting for transfers between devices, body(): lax.all_to_all(send_hist, 'shard', split_axis=0, concat_axis=0, tiled=True)  111 us
    unnamed x3, waiting for transfers between devices  70.2 us
    all_to_all x1, waiting for transfers between devices, body(): lax.all_to_all(send_rows, 'shard', split_axis=0, concat_axis=0, tiled=True)  51.1 us
    psum x1, blocking collectives, body(): grad_score = lax.psum(local_score, ('group', 'shard'))  39.8 us
    all_to_all x1, starting transfers between devices, body(): lax.all_to_all(mentor_output, 'shard', split_axis=0, concat_axis=0, tiled...  28.1 us
    reshape x3, local copies, waits for them, and re-layouts, ranker_block(): key_rows.astype(jnp.bfloat16)  18.5 us
    reshape x3, local copies, waits for them, and re-layouts, ranker_block(): value_rows.astype(jnp.bfloat16)  18.5 us
    dot_general x3, matrix products, ranker_block(): jnp.einsum('skhd,sjhd->shkj', queries, key_rows, preferred_element_type=j...  17.9 us
  transfers between devices with their start and end apart: 6, of which 5 were waited for; matrix products, arithmetic and copies ran while one was open for 4% of the time, Pallas kernels for 0%

commit v1 on v0

--- a/solution.py
+++ b/solution.py
@@ -131,7 +131,7 @@
         tiled=True,
     )
     grad_hidden = lax.psum(grad_rows, "group")
-    grad_score = lax.psum(local_score, ("group", "shard"))
+    grad_score = lax.psum(lax.psum(local_score, axis_name="shard"), axis_name="group")
     return (grad_hidden, grad_score)
 
 

time: 497 us -> 493 us (level)
    psum x1 -> x2, blocking collectives: 39.8 us -> 35 us  [the longest x1 29.5 us: body(): lax.psum(local_score, axis_name='shard')]
where the time goes in v1:
time: 493 us; the launch traced here: 491 us
  waiting for transfers between devices  239 us (48%)
  local copies, waits for them, and re-layouts  77.7 us (16%)
  matrix products  63.9 us (13%)
  starting transfers between devices  56.9 us (12%)
  blocking collectives  35 us (7%)
  between operations  14.2 us (3%)
    all_to_all x1, waiting for transfers between devices, body(): lax.all_to_all(send_hist, 'shard', split_axis=0, concat_axis=0, tiled=True)  111 us
    unnamed x3, waiting for transfers between devices  70.2 us
    all_to_all x1, waiting for transfers between devices, body(): lax.all_to_all(send_rows, 'shard', split_axis=0, concat_axis=0, tiled=True)  51.1 us
    psum x1, blocking collectives, body(): lax.psum(local_score, axis_name='shard')  29.5 us
    all_to_all x1, starting transfers between devices, body(): lax.all_to_all(mentor_output, 'shard', split_axis=0, concat_axis=0, tiled...  28.1 us
    reshape x3, local copies, waits for them, and re-layouts, ranker_block(): key_rows.astype(jnp.bfloat16)  18.5 us
    reshape x3, local copies, waits for them, and re-layouts, ranker_block(): value_rows.astype(jnp.bfloat16)  18.5 us
    dot_general x3, matrix products, ranker_block(): jnp.einsum('skhd,sjhd->shkj', queries, key_rows, preferred_element_type=j...  17.9 us
  transfers between devices with their start and end apart: 6, of which 5 were waited for; matrix products, arithmetic and copies ran while one was open for 4% of the time, Pallas kernels for 0%

profile of v1, /device:TPU:0, one launch (start us, length us, event | category | flops | bytes accessed | tf_op | source)
XLA Modules:
  0.0 490.9 jit_solution(278818853257562)
XLA Ops:
  10.8 7.4 %all-to-all-start.1 = ((bf16[16,3,1]{1,2,0:T(2,128)(2,1)}), bf16[16,3,1]{1,2,0:T(2,128)(2,1)S(1)}, u32[]{:S(2)}, u32[]{:S(2)}) async-start(bf16[16,3,1]{1,2,0:T(2,128)(2,1)} %all_to_all.27), calls=%async_computation.1 | async-start | bytes 16384 | tf_op jit(solution)/shard_map/all_to_all | solution.py:59
  24.6 5.8 %all-to-all-start.2 = ((bf16[48,32,1024]{2,1,0:T(8,128)(2,1)}), bf16[48,32,1024]{2,1,0:T(8,128)(2,1)}, u32[]{:S(2)}, u32[]{:S(2)}) async-start(bf16[48,32,1024]{2,1,0:T(8,128)(2,1)} %copy.50), calls=%async_computation.2 | async-start | bytes 6291456 | tf_op jit(solution)/shard_map/all_to_all | solution.py:57
  32.3 6.3 %copy.47 = bf16[48,128,512]{2,1,0:T(8,128)(2,1)} copy(bf16[48,128,512]{2,0,1:T(8,128)(2,1)S(1)} %convolution_convert_fusion.3) | data formatting | bytes 12582912 | tf_op jit(solution)/shard_map/convert_element_type | solution.py:52
  38.6 51.1 %all-to-all-done.2 = bf16[48,32,1024]{2,1,0:T(8,128)(2,1)} async-done(((bf16[48,32,1024]{2,1,0:T(8,128)(2,1)}), bf16[48,32,1024]{2,1,0:T(8,128)(2,1)}, u32[]{:S(2)}, u32[]{:S(2)}) %all-to-all-start.2) | async-done | bytes 3145760 | tf_op jit(solution)/shard_map/all_to_all | solution.py:57
  89.7 15.5 %all-to-all-start = ((bf16[48,128,512]{2,1,0:T(8,128)(2,1)}), bf16[48,128,512]{2,1,0:T(8,128)(2,1)}, u32[]{:S(2)}, u32[]{:S(2)}) async-start(bf16[48,128,512]{2,1,0:T(8,128)(2,1)} %copy.47), calls=%async_computation | async-start | bytes 12582912 | tf_op jit(solution)/shard_map/all_to_all | solution.py:58
  108.0 111.3 %all-to-all-done = bf16[48,128,512]{2,1,0:T(8,128)(2,1)} async-done(((bf16[48,128,512]{2,1,0:T(8,128)(2,1)}), bf16[48,128,512]{2,1,0:T(8,128)(2,1)}, u32[]{:S(2)}, u32[]{:S(2)}) %all-to-all-start) | async-done | bytes 6291488 | tf_op jit(solution)/shard_map/all_to_all | solution.py:58
  219.3 107.4 %while.10 = (s32[]{:T(128)}, f32[3,16,32]{2,1,0:T(8,128)S(1)}, bf16[3,16,128,512]{3,2,1,0:T(8,128)(2,1)}, bf16[1,512,512]{2,1,0:T(8,128)(2,1)}, bf16[3,16]{1,0:T...) while((s32[]{:T(128)}, f32[3,16,32]{2,1,0:T(8,128)S(1)}, ...), condition=%wide.region_9.10_spmd, body=%wide.region_6.9_spmd.sunk | while | flops 2825123840 | bytes 61932960 | solution.py:98
  225.1 6.2 %reshape.149 = bf16[16,128,8,64]{3,2,1,0:T(8,128)(2,1)} reshape(bf16[2048,512]{1,0:T(8,128)(2,1)} %convolution_convert_fusion.10) | data formatting | bytes 4194304 | tf_op jit(solution)/shard_map/while/body/eval_jaxpr/reshape | solution.py:75
  236.0 6.0 %fusion.64 = (f32[16,8,32]{2,1,0:T(8,128)S(1)}, f32[16,8,32,128]{3,2,1,0:T(8,128)}) fusion(pred[16,128]{1,0:T(8,128)(4,1)S(1)} %iota_compare_fusion.6, bf16[16,128,8,64]{3,2,1,0:T(8,128)(2,1)} %reshape.149, bf16[16,32,8,64]{3,2,1,0:T(8,128)(2,1)S(1)} %reshape.150), kind=kOutput, calls=%fused_computation.9.clone.1 | convolution fusion | flops 68677632 | bytes 4737024 | tf_op jit(solution)/shard_map/while/body/eval_jaxpr/skhd,sjhd->shkj/dot_general | solution.py:82
  244.6 6.2 %reshape.148 = bf16[16,128,8,64]{3,2,1,0:T(8,128)(2,1)} reshape(bf16[2048,512]{1,0:T(8,128)(2,1)} %convolution_convert_fusion.9) | data formatting | bytes 4194304 | tf_op jit(solution)/shard_map/while/body/eval_jaxpr/reshape | solution.py:79
  260.8 6.2 %reshape.149 = bf16[16,128,8,64]{3,2,1,0:T(8,128)(2,1)} reshape(bf16[2048,512]{1,0:T(8,128)(2,1)} %convolution_convert_fusion.10) | data formatting | bytes 4194304 | tf_op jit(solution)/shard_map/while/body/eval_jaxpr/reshape | solution.py:75
  271.8 6.0 %fusion.64 = (f32[16,8,32]{2,1,0:T(8,128)S(1)}, f32[16,8,32,128]{3,2,1,0:T(8,128)}) fusion(pred[16,128]{1,0:T(8,128)(4,1)S(1)} %iota_compare_fusion.6, bf16[16,128,8,64]{3,2,1,0:T(8,128)(2,1)} %reshape.149, bf16[16,32,8,64]{3,2,1,0:T(8,128)(2,1)S(1)} %reshape.150), kind=kOutput, calls=%fused_computation.9.clone.1 | convolution fusion | flops 68677632 | bytes 4737024 | tf_op jit(solution)/shard_map/while/body/eval_jaxpr/skhd,sjhd->shkj/dot_general | solution.py:82
  280.4 6.2 %reshape.148 = bf16[16,128,8,64]{3,2,1,0:T(8,128)(2,1)} reshape(bf16[2048,512]{1,0:T(8,128)(2,1)} %convolution_convert_fusion.9) | data formatting | bytes 4194304 | tf_op jit(solution)/shard_map/while/body/eval_jaxpr/reshape | solution.py:79
  286.6 4.2 multiply_reduce_fusion.5
  296.6 6.2 %reshape.149 = bf16[16,128,8,64]{3,2,1,0:T(8,128)(2,1)} reshape(bf16[2048,512]{1,0:T(8,128)(2,1)} %convolution_convert_fusion.10) | data formatting | bytes 4194304 | tf_op jit(solution)/shard_map/while/body/eval_jaxpr/reshape | solution.py:75
  307.6 6.0 %fusion.64 = (f32[16,8,32]{2,1,0:T(8,128)S(1)}, f32[16,8,32,128]{3,2,1,0:T(8,128)}) fusion(pred[16,128]{1,0:T(8,128)(4,1)S(1)} %iota_compare_fusion.6, bf16[16,128,8,64]{3,2,1,0:T(8,128)(2,1)} %reshape.149, bf16[16,32,8,64]{3,2,1,0:T(8,128)(2,1)S(1)} %reshape.150), kind=kOutput, calls=%fused_computation.9.clone.1 | convolution fusion | flops 68677632 | bytes 4737024 | tf_op jit(solution)/shard_map/while/body/eval_jaxpr/skhd,sjhd->shkj/dot_general | solution.py:82
  316.2 6.2 %reshape.148 = bf16[16,128,8,64]{3,2,1,0:T(8,128)(2,1)} reshape(bf16[2048,512]{1,0:T(8,128)(2,1)} %convolution_convert_fusion.9) | data formatting | bytes 4194304 | tf_op jit(solution)/shard_map/while/body/eval_jaxpr/reshape | solution.py:79
  327.3 28.1 %all-to-all-start.3 = ((f32[16,3,32]{2,1,0:T(4,128)}), f32[16,3,32]{2,1,0:T(4,128)S(1)}, u32[]{:S(2)}, u32[]{:S(2)}) async-start(f32[16,3,32]{2,1,0:T(4,128)} %all_to_all.24), calls=%async_computation.3 | async-start | bytes 65536 | tf_op jit(solution)/shard_map/all_to_all | solution.py:107
  355.5 6.5 %all-to-all-done.3 = f32[16,3,32]{2,1,0:T(4,128)S(1)} async-done(((f32[16,3,32]{2,1,0:T(4,128)}), f32[16,3,32]{2,1,0:T(4,128)S(1)}, u32[]{:S(2)}, u32[]{:S(2)}) %all-to-all-start.3) | async-done | bytes 6176 | tf_op jit(solution)/shard_map/all_to_all | solution.py:107
  362.6 5.2 %convolution_bitcast_fusion = f32[1024,1024]{0,1:T(8,128)} fusion(bf16[512,1024]{1,0:T(8,128)(2,1)} %bitcast.74, f32[512,1024]{1,0:T(8,128)} %get-tuple-element.101, f32[512]{0:T(512)S(1)} %bitcast_subtract_fusion, f32[1024]{0:T(1024)S(1)} %convert_element_type.71), kind=kOutput, calls=%fused_computation.32 | convolution fusion | flops 1075838976 | bytes 7346176 | tf_op jit(solution)/shard_map/dot_general | solution.py:126
  367.8 5.3 %copy.56 = f32[1024,1024]{1,0:T(8,128)} copy(f32[1024,1024]{0,1:T(8,128)} %convolution_bitcast_fusion) | data formatting | bytes 8388608
  373.2 70.1 %reduce-scatter.4.cloned.1.call-done = f32[64,1024]{1,0:T(8,128)} async-done(((f32[1024,1024]{1,0:T(8,128)}), f32[64,1024]{1,0:T(8,128)}) %reduce-scatter.4.cloned.1.call-update) | async-done | bytes 262160
  447.2 29.5 %psum.22 = f32[1024]{0:T(1024)S(1)} all-reduce(f32[1024]{0:T(1024)S(1)} %multiply_reduce_fusion.1), channel_id=1, replica_groups=mesh['group'=2,'shard'=16] {'shard'}, use_global_device_ids=true, to_apply=%region_15.16 | all-reduce | flops 1024 | bytes 8192 | tf_op jit(solution)/shard_map/psum | solution.py:134
  476.7 5.5 %psum.23 = f32[1024]{0:T(1024)} all-reduce(f32[1024]{0:T(1024)S(1)} %psum.22), channel_id=1, replica_groups=mesh['group'=2,'shard'=16] {'group'}, use_global_device_ids=true, to_apply=%region_16.17 | all-reduce | flops 1024 | bytes 8192 | tf_op jit(solution)/shard_map/psum | solution.py:134
  (112 shorter events, 69.8 us)
Async XLA Ops:
  7.2 98.1 %copy-start = (bf16[1024,1024]{1,0:T(8,128)(2,1)S(1)}, bf16[1024,1024]{1,0:T(8,128)(2,1)}, u32[]{:S(2)}) copy-start(bf16[1024,1024]{1,0:T(8,128)(2,1)} %param.18) | copy-start | bytes 6291460
  10.8 13.8 %all-to-all-start.1 = ((bf16[16,3,1]{1,2,0:T(2,128)(2,1)}), bf16[16,3,1]{1,2,0:T(2,128)(2,1)S(1)}, u32[]{:S(2)}, u32[]{:S(2)}) async-start(bf16[16,3,1]{1,2,0:T(2,128)(2,1)} %all_to_all.27), calls=%async_computation.1 | async-start | bytes 16384 | tf_op jit(solution)/shard_map/all_to_all | solution.py:59
  24.2 6.2 %copy-start.4 = (bf16[4,128,512]{2,1,0:T(8,128)(2,1)S(1)}, bf16[4,128,512]{2,1,0:T(8,128)(2,1)}, u32[]{:S(2)}) copy-start(bf16[4,128,512]{2,1,0:T(8,128)(2,1)} %param.17) | copy-start | bytes 1572868
  24.6 65.1 %all-to-all-start.2 = ((bf16[48,32,1024]{2,1,0:T(8,128)(2,1)}), bf16[48,32,1024]{2,1,0:T(8,128)(2,1)}, u32[]{:S(2)}, u32[]{:S(2)}) async-start(bf16[48,32,1024]{2,1,0:T(8,128)(2,1)} %copy.50), calls=%async_computation.2 | async-start | bytes 6291456 | tf_op jit(solution)/shard_map/all_to_all | solution.py:57
  38.6 66.6 %copy-start.7 = (bf16[1024]{0:T(1024)(128)(2,1)S(1)}, bf16[1024]{0:T(1024)(128)(2,1)}, u32[]{:S(2)}) copy-start(bf16[1024]{0:T(1024)(128)(2,1)} %param.19) | copy-start | bytes 6148
  38.6 66.7 %copy-start.3 = (bf16[4,128,1024]{2,1,0:T(8,128)(2,1)S(1)}, bf16[4,128,1024]{2,1,0:T(8,128)(2,1)}, u32[]{:S(2)}) copy-start(bf16[4,128,1024]{2,1,0:T(8,128)(2,1)} %param.13) | copy-start | bytes 3145732
  89.7 129.5 %all-to-all-start = ((bf16[48,128,512]{2,1,0:T(8,128)(2,1)}), bf16[48,128,512]{2,1,0:T(8,128)(2,1)}, u32[]{:S(2)}, u32[]{:S(2)}) async-start(bf16[48,128,512]{2,1,0:T(8,128)(2,1)} %copy.47), calls=%async_computation | async-start | bytes 12582912 | tf_op jit(solution)/shard_map/all_to_all | solution.py:58
  105.3 114.0 %copy-start.5 = (bf16[1,512]{1,0:T(2,128)(2,1)S(1)}, bf16[1,512]{1,0:T(2,128)(2,1)}, u32[]{:S(2)}) copy-start(bf16[1,512]{1,0:T(2,128)(2,1)} %param.23) | copy-start | bytes 3076
  219.3 143.1 %copy-start.6 = (s32[4,32]{1,0:T(4,128)S(1)}, s32[4,32]{1,0:T(4,128)}, u32[]{:S(2)}) copy-start(s32[4,32]{1,0:T(4,128)} %param.14) | copy-start | bytes 1540
  219.3 3.2 copy-start.10
  231.2 1.5 copy-start.8
  236.0 6.0 %copy-start.2 = (bf16[1,16,128,512]{3,2,1,0:T(8,128)(2,1)S(1)}, bf16[1,16,128,512]{3,2,1,0:T(8,128)(2,1)}, u32[]{:S(2)}) copy-start(bf16[1,16,128,512]{3,2,1,0:T(8,128)(2,1)} %copy-done.1) | copy-start | bytes 6291460 | tf_op jit(solution)/shard_map/while
  236.0 6.0 %copy-start.9 = (bf16[1,512,512]{2,1,0:T(8,128)(2,1)S(1)}, bf16[1,512,512]{2,1,0:T(8,128)(2,1)}, u32[]{:S(2)}) copy-start(bf16[1,512,512]{2,1,0:T(8,128)(2,1)} %get-tuple-element.184) | copy-start | bytes 1572868 | tf_op jit(solution)/shard_map/while
  255.1 3.2 copy-start.10
  267.0 1.5 copy-start.8
  271.8 6.0 %copy-start.2 = (bf16[1,16,128,512]{3,2,1,0:T(8,128)(2,1)S(1)}, bf16[1,16,128,512]{3,2,1,0:T(8,128)(2,1)}, u32[]{:S(2)}) copy-start(bf16[1,16,128,512]{3,2,1,0:T(8,128)(2,1)} %copy-done.1) | copy-start | bytes 6291460 | tf_op jit(solution)/shard_map/while
  271.8 6.0 %copy-start.9 = (bf16[1,512,512]{2,1,0:T(8,128)(2,1)S(1)}, bf16[1,512,512]{2,1,0:T(8,128)(2,1)}, u32[]{:S(2)}) copy-start(bf16[1,512,512]{2,1,0:T(8,128)(2,1)} %get-tuple-element.184) | copy-start | bytes 1572868 | tf_op jit(solution)/shard_map/while
  290.9 3.2 copy-start.10
  302.8 1.5 copy-start.8
  307.6 6.0 %copy-start.2 = (bf16[1,16,128,512]{3,2,1,0:T(8,128)(2,1)S(1)}, bf16[1,16,128,512]{3,2,1,0:T(8,128)(2,1)}, u32[]{:S(2)}) copy-start(bf16[1,16,128,512]{3,2,1,0:T(8,128)(2,1)} %copy-done.1) | copy-start | bytes 6291460 | tf_op jit(solution)/shard_map/while
  307.6 6.0 %copy-start.9 = (bf16[1,512,512]{2,1,0:T(8,128)(2,1)S(1)}, bf16[1,512,512]{2,1,0:T(8,128)(2,1)}, u32[]{:S(2)}) copy-start(bf16[1,512,512]{2,1,0:T(8,128)(2,1)} %get-tuple-element.184) | copy-start | bytes 1572868 | tf_op jit(solution)/shard_map/while
  327.3 34.7 %all-to-all-start.3 = ((f32[16,3,32]{2,1,0:T(4,128)}), f32[16,3,32]{2,1,0:T(4,128)S(1)}, u32[]{:S(2)}, u32[]{:S(2)}) async-start(f32[16,3,32]{2,1,0:T(4,128)} %all_to_all.24), calls=%async_computation.3 | async-start | bytes 65536 | tf_op jit(solution)/shard_map/all_to_all | solution.py:107
  355.4 88.0 %reduce-scatter.4.cloned.1.call-start = ((), (), s32[]{:S(2)}) async-start(), calls=%async_computation.6 | async-start | bytes 4456448
  373.1 109.0 %all-reduce.2.cloned.1.call-start = ((), (), s32[]{:S(2)}) async-start(), calls=%async_computation.5 | async-start | bytes 1048576 | tf_op jit(solution)/shard_map/psum | solution.py:133
  (3 other events, 3.9 us)
Sparse Core Ops, SparseCore 0:
  373.3 70.0 reduce-scatter.3
  445.6 27.6 all-reduce.1
